TPU v7x, 256 devices: a whole 4x4x8 slice. The times are simulated.
256 devices in a mesh: dp: 8 (over x, core), ctx: 32 (over y, z).
Axes of the slice: x: 4, y: 4, z: 8, core: 2. Of those that a mesh axis runs over, the one named last changes fastest.
Arguments:
- tile_embed: bfloat16 [8, 32, 512, 1536], P(None, 'ctx', 'dp'), may hold values from -8 to 8
- tile_counts: int32 [8], replicated, may hold values from 4096 to 16384
- w_in: bfloat16 [1536, 768], replicated, may hold values from -1 to 1
- w_qkv: bfloat16 [768, 2304], replicated, may hold values from -1 to 1
- w_out: bfloat16 [768, 768], replicated, may hold values from -0.21875 to 0.21875
Outputs:
- mixed: bfloat16 [8, 16384, 768], P('dp', 'ctx')
Inputs may be any that keep to these rules, and one draw needn't show every extreme that they name: The tissue tiles of slide s fill its first tile_counts[s] positions; the rest are padding.
All inputs are finite; a program needn't handle non-finite values.
Results may differ from a plain program's by a relative error of at most 0.017.
Values may be sent and summed in bfloat16 or wider, within the bound.
A program may use at most 128 MiB of HBM per device.

v0:
```python
import math

import jax
import jax.numpy as jnp
from jax import lax
from jax.sharding import PartitionSpec as P

HEAD_TOTAL = 12


epsilon = 1e-05


def normalize(values):
    average = jnp.mean(values, axis=-1, keepdims=True)
    centered = values - average
    variance = jnp.mean(centered * centered, axis=-1, keepdims=True)
    return (centered * lax.rsqrt(variance + epsilon)).astype(jnp.bfloat16)


def attend_rows(qkv, is_valid):
    length = qkv.shape[0]
    model_features = qkv.shape[1] // 3
    head_width = model_features // HEAD_TOTAL
    key_rows = qkv[:, model_features : 2 * model_features].reshape(length, HEAD_TOTAL, head_width)
    values = qkv[:, 2 * model_features :].reshape(length, HEAD_TOTAL, head_width)
    block_rows = min(length, 512)
    queries = qkv[:, :model_features].reshape(
        length // block_rows, block_rows, HEAD_TOTAL, head_width
    )
    key_mask = is_valid[None, None, :]

    def attend_block(query_rows):
        scores = jnp.einsum(
            "qhd,khd->qhk", query_rows, key_rows, preferred_element_type=jnp.float32
        ) * (1.0 / math.sqrt(head_width))
        running_max = jnp.max(jnp.where(key_mask, scores, -1e30), axis=-1)
        weights = jnp.where(key_mask, jnp.exp(scores - running_max[..., None]), 0.0)
        denominator = jnp.sum(weights, axis=-1)
        weighted = jnp.einsum(
            "qhk,khd->qhd", weights.astype(jnp.bfloat16), values, preferred_element_type=jnp.float32
        )
        return (weighted, running_max, denominator)

    weighted, running_max, denominator = lax.map(attend_block, queries)
    return (
        weighted.reshape(length, HEAD_TOTAL, head_width),
        running_max.reshape(length, HEAD_TOTAL),
        denominator.reshape(length, HEAD_TOTAL),
    )


def body(tile_embed, tile_counts, w_in, w_qkv, w_out):
    slide_id = lax.axis_index("dp")
    ctx_index = lax.axis_index("ctx")
    context_count = lax.axis_size("ctx")
    slide_total, unit_dim, sub_rows, embed_width = tile_embed.shape
    row_count = sub_rows * lax.axis_size("dp")
    model_features = w_out.shape[0]
    head_width = model_features // HEAD_TOTAL
    routed = lax.all_to_all(tile_embed, "dp", split_axis=0, concat_axis=2, tiled=True)
    hidden = jnp.dot(
        routed.reshape(row_count, embed_width), w_in, preferred_element_type=jnp.float32
    ).astype(jnp.bfloat16)
    tile_number = lax.dynamic_slice_in_dim(tile_counts, slide_id, 1)[0]
    positions = ctx_index * row_count + jnp.arange(row_count, dtype=jnp.int32)
    is_valid = positions < tile_number
    normed = normalize(hidden.astype(jnp.float32))
    qkv = jnp.dot(normed, w_qkv, preferred_element_type=jnp.float32).astype(jnp.bfloat16)
    local_accumulator, local_maximum, local_total = attend_rows(qkv, is_valid)
    dilation_step = row_count // context_count
    regrouped = lax.all_to_all(
        qkv.reshape(dilation_step, context_count, 3 * model_features),
        "ctx",
        split_axis=1,
        concat_axis=0,
        tiled=True,
    )
    dilated_branch = regrouped.reshape(row_count, 3 * model_features)
    row_order = jnp.arange(row_count, dtype=jnp.int32)
    dilated_positions = (
        row_order // dilation_step * row_count
        + row_order % dilation_step * context_count
        + ctx_index
    )
    dilated_accumulator, dilated_maximum, dilated_total = attend_rows(
        dilated_branch, dilated_positions < tile_number
    )
    dilated_output = (dilated_accumulator / dilated_total[..., None]).astype(jnp.bfloat16)
    dilated_logsumexp = dilated_maximum + jnp.log(dilated_total)
    restored_output = lax.all_to_all(
        dilated_output.reshape(context_count, dilation_step, 1, model_features),
        "ctx",
        split_axis=0,
        concat_axis=2,
        tiled=True,
    )
    restored_logsumexp = lax.all_to_all(
        dilated_logsumexp.reshape(context_count, dilation_step, 1, HEAD_TOTAL),
        "ctx",
        split_axis=0,
        concat_axis=2,
        tiled=True,
    )
    restored_output = restored_output.reshape(row_count, HEAD_TOTAL, head_width).astype(jnp.float32)
    restored_logsumexp = restored_logsumexp.reshape(row_count, HEAD_TOTAL)
    combined_output = jnp.maximum(local_maximum, restored_logsumexp)
    local_weight = jnp.exp(local_maximum - combined_output)
    dilated_weight = jnp.exp(restored_logsumexp - combined_output)
    attention_fn = (
        local_weight[..., None] * local_accumulator + dilated_weight[..., None] * restored_output
    ) / (local_weight * local_total + dilated_weight)[..., None]
    attention_fn = attention_fn.reshape(row_count, model_features).astype(jnp.bfloat16)
    mixed = jnp.dot(attention_fn, w_out, preferred_element_type=jnp.float32)
    mixed = jnp.where(is_valid[:, None], mixed, 0.0).astype(jnp.bfloat16)
    return mixed.reshape(1, row_count, model_features)


def solution(mesh):
    in_specs = (P(None, "ctx", "dp", None), P(), P(), P(), P())
    out_specs = P("dp", "ctx", None)
    return jax.shard_map(body, mesh=mesh, in_specs=in_specs, out_specs=out_specs, check_vma=False)
```

profile of v0, /device:TPU:1, one launch (start us, length us, event | category | flops | bytes accessed | tf_op | source)
XLA Modules:
  0.0 198.9 jit_solution(5955139675740066602)
XLA Ops:
  0.0 27.6 %all_to_all.48 = bf16[8,1,64,1536]{3,2,1,0:T(8,128)(2,1)S(1)} all-to-all(bf16[8,1,64,1536]{3,2,1,0:T(8,128)(2,1)} %param.5), channel_id=1, replica_groups=mesh['dp'=8,'ctx'=32] {'dp'}, dimensions={0} | all-to-all | bytes 3145728 | tf_op jit(solution)/shard_map/all_to_all | solution.py:61
  27.6 1.5 convert_reduce_fusion
  29.1 0.4 fusion.18
  29.5 2.1 %convolution_convert_fusion = bf16[512,2304]{1,0:T(8,128)(2,1)S(1)} fusion(bf16[768,2304]{1,0:T(8,128)(2,1)S(1)} %copy-done, bf16[512,768]{1,0:T(8,128)(2,1)S(1)} %get-tuple-element.53, f32[512]{0:T(512)S(1)} %add_rsqrt_fusion, f32[512]{0:T(512)S(1)} %broadcast_multiply_fusion), kind=kOutput, calls=%fused_computation.18 | convolution fusion | flops 1814691840 | bytes 6688768 | tf_op jit(solution)/shard_map/dot_general | solution.py:69
  31.6 1.4 copy-done.2
  33.0 2.7 %copy.57 = bf16[16,32,2304]{2,0,1:T(8,128)(2,1)} copy(bf16[16,32,2304]{2,1,0:T(8,128)(2,1)S(1)} %bitcast.99) | data formatting | bytes 4718592 | tf_op jit(solution)/shard_map/reshape | solution.py:73
  35.7 10.6 %all-to-all-start.1 = ((bf16[16,32,2304]{2,0,1:T(8,128)(2,1)}), bf16[16,32,2304]{2,0,1:T(8,128)(2,1)}, u32[]{:S(2)}, u32[]{:S(2)}) async-start(bf16[16,32,2304]{2,0,1:T(8,128)(2,1)} %copy.57), calls=%async_computation.1 | async-start | bytes 4718592 | tf_op jit(solution)/shard_map/all_to_all | solution.py:72
  46.3 0.6 dynamic_slice.8
  46.9 0.7 fusion.40
  47.6 3.1 %fusion.51 = (bf16[512,768]{1,0:T(8,128)(2,1)}, bf16[512,768]{1,0:T(8,128)(2,1)}, bf16[512,768]{1,0:T(8,128)(2,1)}) fusion(bf16[512,2304]{1,0:T(8,128)(2,1)} %copy-done.2), kind=kLoop, calls=%fused_computation.67 | loop fusion | bytes 4718592 | tf_op jit(solution)/shard_map/slice | solution.py:28
  50.7 2.3 %copy.55 = bf16[512,768]{0,1:T(8,128)(2,1)} copy(bf16[512,768]{1,0:T(8,128)(2,1)} %get-tuple-element.48) | data formatting | bytes 1572864 | tf_op jit(solution)/shard_map/slice | solution.py:25
  53.0 2.4 %copy.56 = bf16[512,768]{0,1:T(8,128)(2,1)} copy(bf16[512,768]{1,0:T(8,128)(2,1)} %get-tuple-element.38) | data formatting | bytes 1572864 | tf_op jit(solution)/shard_map/slice | solution.py:28
  55.4 9.4 %fusion.3 = (f32[512,12]{0,1:T(8,128)}, f32[12,512,512]{2,1,0:T(8,128)}) fusion(pred[512]{0:T(512)(128)(4,1)S(1)} %get-tuple-element.69, bf16[512,12,64]{0,2,1:T(8,128)(2,1)} %bitcast.102, bf16[512,12,64]{0,2,1:T(8,128)(2,1)} %bitcast.104), kind=kOutput, calls=%fused_computation.7 | convolution fusion | flops 412084224 | bytes 14180864 | tf_op jit(solution)/shard_map/while/body/eval_jaxpr/qhd,khd->qhk/dot_general | solution.py:34
  64.8 35.5 %all-to-all-done.1 = bf16[16,32,2304]{2,0,1:T(8,128)(2,1)} async-done(((bf16[16,32,2304]{2,0,1:T(8,128)(2,1)}), bf16[16,32,2304]{2,0,1:T(8,128)(2,1)}, u32[]{:S(2)}, u32[]{:S(2)}) %all-to-all-start.1) | async-done | bytes 2359328 | tf_op jit(solution)/shard_map/all_to_all | solution.py:72
  100.3 3.1 %fusion.52 = (bf16[512,768]{1,0:T(8,128)(2,1)}, bf16[512,768]{1,0:T(8,128)(2,1)}, bf16[512,768]{1,0:T(8,128)(2,1)}) fusion(bf16[512,2304]{1,0:T(8,128)(2,1)} %bitcast.8), kind=kLoop, calls=%fused_computation.68 | loop fusion | bytes 4718592 | tf_op jit(solution)/shard_map/slice | solution.py:28
  103.4 2.3 %copy.64 = bf16[512,768]{0,1:T(8,128)(2,1)} copy(bf16[512,768]{1,0:T(8,128)(2,1)} %get-tuple-element.50) | data formatting | bytes 1572864 | tf_op jit(solution)/shard_map/slice | solution.py:26
  105.7 2.3 %copy.58 = bf16[512,768]{0,1:T(8,128)(2,1)} copy(bf16[512,768]{1,0:T(8,128)(2,1)} %get-tuple-element.51) | data formatting | bytes 1572864 | tf_op jit(solution)/shard_map/slice | solution.py:25
  108.0 2.3 %copy.59 = bf16[512,768]{0,1:T(8,128)(2,1)} copy(bf16[512,768]{1,0:T(8,128)(2,1)} %get-tuple-element.49) | data formatting | bytes 1572864 | tf_op jit(solution)/shard_map/slice | solution.py:28
  110.3 4.3 %fusion = (f32[512,12]{0,1:T(8,128)S(1)}, f32[12,512,512]{2,1,0:T(8,128)S(1)}) fusion(pred[512]{0:T(512)(128)(4,1)S(1)} %get-tuple-element.68, bf16[512,12,64]{0,2,1:T(8,128)(2,1)} %bitcast.101, bf16[512,12,64]{0,2,1:T(8,128)(2,1)} %bitcast.103), kind=kOutput, calls=%fused_computation.2 | convolution fusion | flops 412084224 | bytes 14180864 | tf_op jit(solution)/shard_map/while/body/eval_jaxpr/qhd,khd->qhk/dot_general | solution.py:34
  114.7 2.6 %fusion.9 = f32[512,12]{0,1:T(8,128)S(1)} fusion(f32[12,512,512]{2,1,0:T(8,128)S(1)} %get-tuple-element.55, f32[512,12]{0,1:T(8,128)S(1)} %get-tuple-element.54, pred[512]{0:T(512)(128)(4,1)S(1)} %get-tuple-element.68), kind=kLoop, calls=%fused_computation.13 | loop fusion | flops 12576768 | bytes 12632576 | tf_op jit(solution)/shard_map/while/body/eval_jaxpr/reduce_sum | solution.py:39
  117.2 1.9 copy-done.1
  119.1 0.0 copy-done.3
  119.1 0.6 copy-done.4
  119.7 0.6 log_add_fusion
  120.3 1.5 add.98
  121.9 1.8 copy.74
  123.7 0.5 broadcast.137
  124.2 2.7 %reduce = f32[32,12,16]{2,1,0:T(8,128)} reduce(f32[32,12,1,16]{3,2,1,0:T(1,128)} %bitcast.109, f32[]{:T(128)} %broadcast.137), dimensions={2}, to_apply=%bitcast.98.reduce_sub_computation | reduce | bytes 49156
  126.9 1.7 reshape.206
  128.6 7.6 %all-to-all-start.2 = ((f32[32,1,192]{2,1,0:T(1,128)}), f32[32,1,192]{2,1,0:T(1,128)}, u32[]{:S(2)}, u32[]{:S(2)}) async-start(f32[32,1,192]{2,1,0:T(1,128)} %reshape.206), calls=%async_computation.2 | async-start | bytes 65536 | tf_op jit(solution)/shard_map/all_to_all | solution.py:98
  136.2 8.0 %fusion.21 = bf16[512,12,64]{0,2,1:T(8,128)(2,1)} fusion(bf16[512,12,64]{0,2,1:T(8,128)(2,1)} %bitcast.107, f32[12,512,512]{2,1,0:T(8,128)} %copy-done.1, f32[512,12]{0,1:T(8,128)} %copy-done.3, pred[512]{0:T(512)(128)(4,1)S(1)} %get-tuple-element.68, f32[512,12]{0,1:T(8,128)} %copy-done.4), kind=kOutput, calls=%fused_computation.28 | convolution fusion | flops 416022528 | bytes 14205440 | tf_op jit(solution)/shard_map/while/body/eval_jaxpr/qhk,khd->qhd/dot_general | solution.py:40
  144.2 3.8 %copy.66 = bf16[512,12,64]{2,1,0:T(8,128)(2,1)} copy(bf16[512,12,64]{0,2,1:T(8,128)(2,1)} %fusion.21) | data formatting | bytes 1572864 | tf_op jit(solution)/shard_map/convert_element_type | solution.py:89
  147.9 3.9 %convert_element_type.59 = bf16[32,16,1,768]{3,1,0,2:T(8,128)(2,1)} reshape(bf16[512,12,64]{2,1,0:T(8,128)(2,1)} %copy.66) | data formatting | bytes 1572864 | tf_op jit(solution)/shard_map/convert_element_type | solution.py:89
  151.8 9.1 %all-to-all-start.3 = ((bf16[32,16,1,768]{3,1,2,0:T(8,128)(2,1)}), bf16[32,16,1,768]{3,1,2,0:T(8,128)(2,1)}, u32[]{:S(2)}, u32[]{:S(2)}) async-start(bf16[32,16,1,768]{3,1,2,0:T(8,128)(2,1)} %bitcast.105), calls=%async_computation.3 | async-start | bytes 1572864 | tf_op jit(solution)/shard_map/all_to_all | solution.py:91
  160.9 7.7 %fusion.6 = f32[512,12]{0,1:T(8,128)} fusion(f32[12,512,512]{2,1,0:T(8,128)} %get-tuple-element.66, f32[512,12]{0,1:T(8,128)} %get-tuple-element.64, pred[512]{0:T(512)(128)(4,1)S(1)} %get-tuple-element.69), kind=kLoop, calls=%fused_computation.10 | loop fusion | flops 12576768 | bytes 12632576 | tf_op jit(solution)/shard_map/while/body/eval_jaxpr/reduce_sum | solution.py:39
  168.6 2.3 %copy.62 = bf16[512,768]{0,1:T(8,128)(2,1)} copy(bf16[512,768]{1,0:T(8,128)(2,1)} %get-tuple-element.39) | data formatting | bytes 1572864 | tf_op jit(solution)/shard_map/slice | solution.py:26
  170.9 2.0 %reduce.1 = f32[32,192]{1,0:T(8,128)} reduce(f32[32,1,192]{2,1,0:T(1,128)} %all-to-all-done.2, f32[]{:T(128)} %broadcast.137), dimensions={1}, to_apply=%all_to_all.40.reduce_sub_computation | reduce | bytes 49156 | tf_op jit(solution)/shard_map/all_to_all | solution.py:98
  172.9 1.8 reshape.207
  174.6 1.6 bitcast_bitcast_fusion
  176.3 1.7 copy.61
  177.9 1.6 reshape.200
  179.5 1.4 multiply_add_fusion
  181.0 8.2 %bitcast_multiply_fusion.1 = f32[512,12,64]{0,2,1:T(8,128)} fusion(bf16[512,12,64]{0,2,1:T(8,128)(2,1)} %bitcast.108, f32[12,512,512]{2,1,0:T(8,128)} %get-tuple-element.66, f32[512,12]{0,1:T(8,128)} %get-tuple-element.64, pred[512]{0:T(512)(128)(4,1)S(1)} %get-tuple-element.69, f32[512,12]{0,1:T(8,128)S(1)} %get-tuple-element.37), kind=kOutput, calls=%fused_computation.31 | convolution fusion | flops 415629312 | bytes 14991872 | tf_op jit(solution)/shard_map/while/body/eval_jaxpr/qhk,khd->qhd/dot_general | solution.py:40
  189.2 0.0 all-to-all-done.3
  189.2 2.5 %bitcast_convert_fusion = f32[32,1,16,1,768]{4,0,2,3,1:T(8,128)} fusion(bf16[32,16,1,768]{3,1,2,0:T(8,128)(2,1)} %all-to-all-done.3), kind=kLoop, calls=%fused_computation.35 | loop fusion | flops 393216 | bytes 2359296 | tf_op jit(solution)/shard_map/convert_element_type | solution.py:105
  191.7 3.0 %copy.69 = f32[512,768]{0,1:T(8,128)} copy(f32[512,768]{1,0:T(8,128)} %bitcast.100) | data formatting | bytes 3145728 | tf_op jit(solution)/shard_map/convert_element_type | solution.py:105
  194.8 2.4 %fusion.20 = bf16[512,768]{0,1:T(8,128)(2,1)S(1)} fusion(f32[512,768]{0,1:T(8,128)} %copy.69, f32[512,12,64]{0,2,1:T(8,128)} %bitcast_multiply_fusion.1, f32[512,12]{0,1:T(8,128)} %get-tuple-element.35, f32[512,12]{0,1:T(8,128)} %get-tuple-element.36), kind=kLoop, calls=%fused_computation.26 | loop fusion | flops 1572864 | bytes 3981312 | tf_op jit(solution)/shard_map/convert_element_type | solution.py:113
  197.2 1.7 fusion.27
  (15 shorter events, 0.0 us)
Async XLA Ops:
  0.0 29.5 %copy-start = (bf16[768,2304]{1,0:T(8,128)(2,1)S(1)}, bf16[768,2304]{1,0:T(8,128)(2,1)}, u32[]{:S(2)}) copy-start(bf16[768,2304]{1,0:T(8,128)(2,1)} %param.8) | copy-start | bytes 10616836
  0.0 27.6 %copy-start.5 = (bf16[1536,768]{1,0:T(8,128)(2,1)S(1)}, bf16[1536,768]{1,0:T(8,128)(2,1)}, u32[]{:S(2)}) copy-start(bf16[1536,768]{1,0:T(8,128)(2,1)} %param.7) | copy-start | bytes 7077892
  31.6 1.4 copy-start.2
  35.7 10.6 %copy-start.7 = (s32[8]{0:T(128)S(1)}, s32[8]{0:T(128)}, u32[]{:S(2)}) copy-start(s32[8]{0:T(128)} %param.6) | copy-start | bytes 100
  35.7 64.6 %all-to-all-start.1 = ((bf16[16,32,2304]{2,0,1:T(8,128)(2,1)}), bf16[16,32,2304]{2,0,1:T(8,128)(2,1)}, u32[]{:S(2)}, u32[]{:S(2)}) async-start(bf16[16,32,2304]{2,0,1:T(8,128)(2,1)} %copy.57), calls=%async_computation.1 | async-start | bytes 4718592 | tf_op jit(solution)/shard_map/all_to_all | solution.py:72
  114.6 4.5 %copy-start.1 = (f32[12,512,512]{2,1,0:T(8,128)}, f32[12,512,512]{2,1,0:T(8,128)S(1)}, u32[]{:S(2)}) copy-start(f32[12,512,512]{2,1,0:T(8,128)S(1)} %get-tuple-element.55) | copy-start | bytes 37748740
  114.6 4.5 %copy-start.3 = (f32[512,12]{0,1:T(8,128)}, f32[512,12]{0,1:T(8,128)S(1)}, u32[]{:S(2)}) copy-start(f32[512,12]{0,1:T(8,128)S(1)} %get-tuple-element.54) | copy-start | bytes 73732
  119.1 0.6 copy-start.4
  128.6 23.2 %all-to-all-start.2 = ((f32[32,1,192]{2,1,0:T(1,128)}), f32[32,1,192]{2,1,0:T(1,128)}, u32[]{:S(2)}, u32[]{:S(2)}) async-start(f32[32,1,192]{2,1,0:T(1,128)} %reshape.206), calls=%async_computation.2 | async-start | bytes 65536 | tf_op jit(solution)/shard_map/all_to_all | solution.py:98
  151.8 37.4 %all-to-all-start.3 = ((bf16[32,16,1,768]{3,1,2,0:T(8,128)(2,1)}), bf16[32,16,1,768]{3,1,2,0:T(8,128)(2,1)}, u32[]{:S(2)}, u32[]{:S(2)}) async-start(bf16[32,16,1,768]{3,1,2,0:T(8,128)(2,1)} %bitcast.105), calls=%async_computation.3 | async-start | bytes 1572864 | tf_op jit(solution)/shard_map/all_to_all | solution.py:91
  194.8 2.4 %copy-start.6 = (bf16[768,768]{1,0:T(8,128)(2,1)S(1)}, bf16[768,768]{1,0:T(8,128)(2,1)}, u32[]{:S(2)}) copy-start(bf16[768,768]{1,0:T(8,128)(2,1)} %param.9) | copy-start | bytes 3538948
where the time goes:
time: 201 us; the launch traced here: 199 us
  local copies, waits for them, and re-layouts  50.2 us (25%)
  waiting for transfers between devices  35.6 us (18%)
  matrix products  35.2 us (18%)
  blocking collectives  27.6 us (14%)
  starting transfers between devices  27.3 us (14%)
  other arithmetic  23 us (11%)
    all_to_all x1, waiting for transfers between devices, body(): lax.all_to_all(qkv.reshape(dilation_step, context_count, 3 * model_featur...  35.5 us
    all_to_all x1, blocking collectives, body(): lax.all_to_all(tile_embed, 'dp', split_axis=0, concat_axis=2, tiled=True)  27.6 us
    dot_general x2, matrix products, attend_block(): jnp.einsum('qhk,khd->qhd', weights.astype(jnp.bfloat16), values, preferre...  16.2 us
    dot_general x2, matrix products, attend_block(): jnp.einsum('qhd,khd->qhk', query_rows, key_rows, preferred_element_type=j...  13.7 us
    slice x4, local copies, waits for them, and re-layouts, attend_rows(): qkv[:, :model_features]  10.8 us
    all_to_all x1, starting transfers between devices, body(): lax.all_to_all(qkv.reshape(dilation_step, context_count, 3 * model_featur...  10.6 us
    reduce_sum x2, other arithmetic, attend_block(): denominator = jnp.sum(weights, axis=-1)  10.3 us
    all_to_all x1, starting transfers between devices, body(): lax.all_to_all(dilated_output.reshape(context_count, dilation_step, 1, mo...  9.06 us
  transfers between devices with their start and end apart: 3, of which 1 were waited for; matrix products, arithmetic and copies ran while one was open for 31% of the time, Pallas kernels for 0%

commit v1 on v0

v1 whole, which is shorter than its diff:
```python
import functools
import math

import jax
import jax.numpy as jnp
from jax import lax
from jax.experimental import pallas as pl
from jax.experimental.pallas import tpu as pltpu
from jax.sharding import PartitionSpec as P

HEAD_TOTAL = 12
HEAD = 64
epsilon = 1e-05
LOG2E = 1.4426950408889634
QB = 256


def project(x, w_ref, valid, q_ref, k_ref, v_ref):
    feat = x.shape[1]
    scale = LOG2E / math.sqrt(HEAD)
    for t in range(feat // 256):
        cols = pl.ds(t * 256, 256)
        q = jnp.dot(x, w_ref[:, pl.ds(t * 256, 256)], preferred_element_type=jnp.float32)
        q_ref[:, cols] = (q * scale).astype(jnp.bfloat16)
        k = jnp.dot(x, w_ref[:, pl.ds(feat + t * 256, 256)], preferred_element_type=jnp.float32)
        k_ref[:, cols] = jnp.where(valid, k, k[0:1, :]).astype(jnp.bfloat16)
        v = jnp.dot(x, w_ref[:, pl.ds(2 * feat + t * 256, 256)], preferred_element_type=jnp.float32)
        v_ref[:, cols] = jnp.where(valid, v, 0.0).astype(jnp.bfloat16)


def attend_pair(q_ref, k_ref, v_ref, ones, pair, rows):
    low = lax.broadcasted_iota(jnp.int32, (1, 128), 1) < HEAD
    cols = pl.ds(pair * 128, 128)
    q = q_ref[rows, cols]
    k = k_ref[:, cols]
    v = jnp.concatenate([v_ref[:, cols], ones], axis=1)
    res = []
    for half in range(2):
        pick = low if half == 0 else jnp.logical_not(low)
        km = jnp.where(pick, k, jnp.zeros_like(k))
        s = lax.dot_general(q, km, (((1,), (1,)), ((), ())), preferred_element_type=jnp.float32)
        m = jnp.max(s, axis=1, keepdims=True)
        p = jnp.exp2(s - m).astype(jnp.bfloat16)
        o = jnp.dot(p, v, preferred_element_type=jnp.float32)
        res.append((o[:, :128], o[:, 128:], m))
    (a0, l0, m0), (a1, l1, m1) = res
    a = jnp.where(low, a0, a1)
    l = jnp.where(low, l0, l1)
    lse0 = m0 + jnp.log2(l0)
    lse1 = m1 + jnp.log2(l1)
    return a / l, lse0, lse1


def attn_kernel(n_ref, x_ref, w_ref, out_ref, lse_ref, q_ref, k_ref, v_ref):
    rows_total = x_ref.shape[0]
    n = n_ref[0]
    row = lax.broadcasted_iota(jnp.int32, (rows_total, 1), 0)
    valid = row < n
    project(x_ref[...], w_ref, valid, q_ref, k_ref, v_ref)
    ones = jnp.where(lax.broadcasted_iota(jnp.int32, (rows_total, 128), 0) < n, 1.0, 0.0).astype(jnp.bfloat16)
    lane = lax.broadcasted_iota(jnp.int32, (1, 128), 1)
    for b in range(rows_total // QB):
        rows = pl.ds(b * QB, QB)
        acc = jnp.zeros((QB, 128), jnp.float32)
        for pair in range(HEAD_TOTAL // 2):
            o, lse0, lse1 = attend_pair(q_ref, k_ref, v_ref, ones, pair, rows)
            out_ref[rows, pl.ds(pair * 128, 128)] = o.astype(out_ref.dtype)
            acc = jnp.where(lane == 2 * pair, lse0, acc)
            acc = jnp.where(lane == 2 * pair + 1, lse1, acc)
        lse_ref[rows, :] = acc


def attention(n, x, w_qkv, out_dtype):
    rows, feat = x.shape
    return pl.pallas_call(
        attn_kernel,
        out_shape=(
            jax.ShapeDtypeStruct((rows, feat), out_dtype),
            jax.ShapeDtypeStruct((rows, 128), jnp.float32),
        ),
        in_specs=[
            pl.BlockSpec(memory_space=pltpu.SMEM),
            pl.BlockSpec(memory_space=pltpu.VMEM),
            pl.BlockSpec(memory_space=pltpu.VMEM),
        ],
        out_specs=(pl.BlockSpec(memory_space=pltpu.VMEM), pl.BlockSpec(memory_space=pltpu.VMEM)),
        scratch_shapes=[pltpu.VMEM((rows, feat), jnp.bfloat16)] * 3,
        cost_estimate=pl.CostEstimate(
            flops=2 * rows * feat * 3 * feat + 4 * rows * rows * feat * 4,
            bytes_accessed=rows * feat * 20,
            transcendentals=rows * rows * HEAD_TOTAL,
        ),
    )(n, x, w_qkv)


def body(tile_embed, tile_counts, w_in, w_qkv, w_out):
    slide_id = lax.axis_index("dp")
    ctx_index = lax.axis_index("ctx")
    context_count = lax.axis_size("ctx")
    slide_total, _, sub_rows, embed_width = tile_embed.shape
    row_count = sub_rows * lax.axis_size("dp")
    feat = w_out.shape[0]
    steps = row_count // context_count
    hidden = jnp.dot(
        tile_embed.reshape(slide_total * sub_rows, embed_width), w_in, preferred_element_type=jnp.float32
    ).astype(jnp.bfloat16).astype(jnp.float32)
    average = jnp.mean(hidden, axis=-1, keepdims=True)
    centered = hidden - average
    variance = jnp.mean(centered * centered, axis=-1, keepdims=True)
    normed = (centered * lax.rsqrt(variance + epsilon)).astype(jnp.bfloat16)
    routed = lax.all_to_all(
        normed.reshape(slide_total, sub_rows, feat), "dp", split_axis=0, concat_axis=0, tiled=True
    ).reshape(row_count, feat)
    tile_number = lax.dynamic_slice_in_dim(tile_counts, slide_id, 1)
    grouped = routed.reshape(steps, context_count, feat).transpose(1, 0, 2)
    dil = lax.all_to_all(grouped, "ctx", split_axis=0, concat_axis=0, tiled=True).reshape(row_count, feat)
    n_local = jnp.clip(tile_number - ctx_index * row_count, 1, row_count)
    n_dil = jnp.clip((tile_number - ctx_index + context_count - 1) // context_count, 1, row_count)
    out_l, lse_l = attention(n_local, routed, w_qkv, jnp.float32)
    out_d, lse_d = attention(n_dil, dil, w_qkv, jnp.bfloat16)
    back = lax.all_to_all(
        out_d.reshape(context_count, steps, feat), "ctx", split_axis=0, concat_axis=0, tiled=True
    )
    back_lse = lax.all_to_all(
        lse_d[:, :16].reshape(context_count, 2, 128), "ctx", split_axis=0, concat_axis=0, tiled=True
    ).reshape(context_count, steps, 16)
    back = back.transpose(1, 0, 2).reshape(row_count, feat).astype(jnp.float32)
    back_lse = back_lse.transpose(1, 0, 2).reshape(row_count, 16)[:, :HEAD_TOTAL]
    share = 1.0 / (1.0 + jnp.exp2(lse_l[:, :HEAD_TOTAL] - back_lse))
    share = jnp.repeat(share, HEAD, axis=1)
    attn = (out_l + share * (back - out_l)).astype(jnp.bfloat16)
    mixed = jnp.dot(attn, w_out, preferred_element_type=jnp.float32)
    positions = ctx_index * row_count + jnp.arange(row_count, dtype=jnp.int32)
    mixed = jnp.where((positions < tile_number[0])[:, None], mixed, 0.0).astype(jnp.bfloat16)
    return mixed.reshape(1, row_count, feat)


def solution(mesh):
    in_specs = (P(None, "ctx", "dp", None), P(), P(), P(), P())
    out_specs = P("dp", "ctx", None)
    return jax.shard_map(body, mesh=mesh, in_specs=in_specs, out_specs=out_specs, check_vma=False)
```

time: 201 us -> 114 us (0.57)
  the two profiles are of different devices: /device:TPU:1 before, /device:TPU:32 now
where the time goes in v1:
time: 114 us; the launch traced here: 113 us
  blocking collectives  30.8 us (27%)
  waiting for transfers between devices  24.9 us (22%)
  Pallas kernels  18.6 us (16%)
  starting transfers between devices  16.3 us (14%)
  local copies, waits for them, and re-layouts  13.2 us (12%)
  matrix products  4.53 us (4%)
  other arithmetic  3.51 us (3%)
  between operations  1.41 us (1%)
    all_to_all x1, waiting for transfers between devices, body(): lax.all_to_all(grouped, 'ctx', split_axis=0, concat_axis=0, tiled=True)  21.6 us
    pallas_call x2, Pallas kernels, attention(): pl.pallas_call(attn_kernel, out_shape=(jax.ShapeDtypeStruct((rows, feat),...  18.6 us
    all_to_all x1, blocking collectives, body(): lax.all_to_all(normed.reshape(slide_total, sub_rows, feat), 'dp', split_a...  17.3 us
    all_to_all x1, blocking collectives, body(): lax.all_to_all(lse_d[:, :16].reshape(context_count, 2, 128), 'ctx', split...  13.6 us
    all_to_all x1, starting transfers between devices, body(): lax.all_to_all(grouped, 'ctx', split_axis=0, concat_axis=0, tiled=True)  11.4 us
    all_to_all x1, starting transfers between devices, body(): lax.all_to_all(out_d.reshape(context_count, steps, feat), 'ctx', split_ax...  4.89 us
    unnamed x12, local copies, waits for them, and re-layouts  3.57 us
    all_to_all x1, waiting for transfers between devices, body(): lax.all_to_all(out_d.reshape(context_count, steps, feat), 'ctx', split_ax...  3.34 us
  transfers between devices with their start and end apart: 2, of which 2 were waited for; matrix products, arithmetic and copies ran while one was open for 8% of the time, Pallas kernels for 8%

profile of v1, /device:TPU:32, one launch (start us, length us, event | category | flops | bytes accessed | tf_op | source)
XLA Modules:
  0.0 113.3 jit_solution(10193725496316308730)
XLA Ops:
  0.0 0.0 copy-start
  0.0 1.7 %copy-done = bf16[1536,768]{1,0:T(8,128)(2,1)S(1)} copy-done((bf16[1536,768]{1,0:T(8,128)(2,1)S(1)}, bf16[1536,768]{1,0:T(8,128)(2,1)}, u32[]{:S(2)}) %copy-start) | copy-done | bytes 2359320
  1.7 2.9 %convert_reduce_fusion = (f32[512]{0:T(512)S(1)}, bf16[512,768]{1,0:T(8,128)(2,1)S(1)}) fusion(bf16[512,1536]{1,0:T(8,128)(2,1)} %bitcast.41, bf16[1536,768]{1,0:T(8,128)(2,1)S(1)} %copy-done), kind=kOutput, calls=%fused_computation.1 | convolution fusion | flops 1209138688 | bytes 4720640 | tf_op jit(solution)/shard_map/dot_general | solution.py:104
  4.5 0.4 fusion.2
  4.9 0.3 fusion.3
  5.2 17.3 %all_to_all.20 = bf16[8,64,768]{2,1,0:T(8,128)(2,1)S(1)} all-to-all(bf16[8,64,768]{2,1,0:T(8,128)(2,1)S(1)} %bitcast.36), channel_id=1, replica_groups=mesh['dp'=8,'ctx'=32] {'dp'}, dimensions={0} | all-to-all | bytes 1572864 | tf_op jit(solution)/shard_map/all_to_all | solution.py:111
  22.5 0.0 copy-start.2
  22.5 0.0 copy-start.5
  22.5 1.3 %copy.20 = bf16[32,16,768]{2,1,0:T(8,128)(2,1)} copy(bf16[32,16,768]{2,0,1:T(8,128)(2,1)S(1)} %bitcast.34) | data formatting | bytes 1572864 | tf_op jit(solution)/shard_map/transpose | solution.py:115
  23.8 0.0 copy-done.2
  23.8 11.4 %all-to-all-start.1 = ((bf16[32,16,768]{2,1,0:T(8,128)(2,1)}), bf16[32,16,768]{2,1,0:T(8,128)(2,1)}, u32[]{:S(2)}, u32[]{:S(2)}) async-start(bf16[32,16,768]{2,1,0:T(8,128)(2,1)} %copy.20), calls=%async_computation.1 | async-start | bytes 1572864 | tf_op jit(solution)/shard_map/all_to_all | solution.py:116
  35.2 0.0 copy-done.5
  35.2 0.6 dynamic_slice.3
  36.5 21.6 %all-to-all-done.1 = bf16[32,16,768]{2,1,0:T(8,128)(2,1)} async-done(((bf16[32,16,768]{2,1,0:T(8,128)(2,1)}), bf16[32,16,768]{2,1,0:T(8,128)(2,1)}, u32[]{:S(2)}, u32[]{:S(2)}) %all-to-all-start.1) | async-done | bytes 786464 | tf_op jit(solution)/shard_map/all_to_all | solution.py:116
  58.1 9.2 %shard_map.56 = (bf16[512,768]{1,0:T(8,128)(2,1)}, f32[512,128]{1,0:T(8,128)}) custom-call(s32[1]{0:T(128)S(6)} %min.11.n_ref, bf16[512,768]{1,0:T(8,128)(2,1)} %bitcast.8.x_ref, bf16[768,2304]{1,0:T(8,128)(2,1)} %w_ref.3), custom_call_target="tpu_custom_call" | custom-call | flops 5033164800 | bytes 7864320 | tf_op jit(solution)/shard_map/pallas_call | solution.py:75
  67.3 1.1 reshape.58
  68.4 13.6 %all_to_all.21 = f32[32,2,128]{2,1,0:T(2,128)S(1)} all-to-all(f32[32,2,128]{2,1,0:T(2,128)S(1)} %reshape.58), channel_id=1, replica_groups=mesh['dp'=8,'ctx'=32] {'ctx'}, dimensions={0} | all-to-all | bytes 65536 | tf_op jit(solution)/shard_map/all_to_all | solution.py:124
  81.9 4.9 %all-to-all-start.3 = ((bf16[32,16,768]{2,1,0:T(8,128)(2,1)}), bf16[32,16,768]{2,1,0:T(8,128)(2,1)S(1)}, u32[]{:S(2)}, u32[]{:S(2)}) async-start(bf16[32,16,768]{2,1,0:T(8,128)(2,1)} %bitcast.38), calls=%async_computation.3 | async-start | bytes 1572864 | tf_op jit(solution)/shard_map/all_to_all | solution.py:121
  87.5 0.6 add_compare_fusion
  88.1 9.4 %shard_map.55 = (f32[512,768]{1,0:T(8,128)}, f32[512,128]{1,0:T(8,128)}) custom-call(s32[1]{0:T(128)S(6)} %min.10.n_ref, bf16[512,768]{1,0:T(8,128)(2,1)} %bitcast.35, bf16[768,2304]{1,0:T(8,128)(2,1)} %w_ref.3), custom_call_target="tpu_custom_call" | custom-call | flops 5033164800 | bytes 7864320 | tf_op jit(solution)/shard_map/pallas_call | solution.py:75
  97.6 0.1 copy.21
  97.7 0.1 copy.22
  97.8 1.7 %fusion.11 = f32[512,12]{1,0:T(8,128)} fusion(f32[512,16]{1,0:T(8,128)S(1)} %bitcast.37, f32[512,128]{1,0:T(8,128)} %get-tuple-element.10), kind=kLoop, calls=%fused_computation.18 | loop fusion | flops 24576 | bytes 73728 | tf_op jit(solution)/shard_map/div | solution.py:129
  99.5 1.1 copy.25
  100.6 1.4 %broadcast_in_dim.19 = f32[512,12,64]{0,2,1:T(8,128)} broadcast(f32[512,12]{0,1:T(8,128)S(1)} %copy.25), dimensions={0,1} | broadcast | bytes 1597440 | tf_op jit(solution)/shard_map/broadcast_in_dim | solution.py:130
  102.0 3.0 %copy.27 = f32[512,768]{1,0:T(8,128)} copy(f32[512,768]{0,1:T(8,128)} %bitcast.33) | data formatting | bytes 3145728 | tf_op jit(solution)/shard_map/reshape | solution.py:130
  105.0 3.3 %all-to-all-done.3 = bf16[32,16,768]{2,1,0:T(8,128)(2,1)S(1)} async-done(((bf16[32,16,768]{2,1,0:T(8,128)(2,1)}), bf16[32,16,768]{2,1,0:T(8,128)(2,1)S(1)}, u32[]{:S(2)}, u32[]{:S(2)}) %all-to-all-start.3) | async-done | bytes 786464 | tf_op jit(solution)/shard_map/all_to_all | solution.py:121
  108.3 0.2 convert_bitcast_fusion
  108.5 0.0 copy-start.1
  108.5 0.0 copy-start.3
  108.5 0.9 copy.26
  109.4 0.5 copy-done.1
  109.9 0.5 copy-done.3
  110.4 0.0 copy-start.4
  110.4 0.3 fusion.6
  110.7 1.0 copy-done.4
  111.7 1.7 %fusion.7 = bf16[1,512,768]{2,1,0:T(8,128)(2,1)} fusion(bf16[512,768]{1,0:T(8,128)(2,1)S(1)} %fusion.6, bf16[768,768]{1,0:T(8,128)(2,1)S(1)} %copy-done.4, pred[512]{0:T(512)(128)(4,1)S(1)} %add_compare_fusion), kind=kOutput, calls=%fused_computation.13 | convolution fusion | flops 604766208 | bytes 2753024 | tf_op jit(solution)/shard_map/dot_general | solution.py:132
  (2 shorter events, 0.0 us)
Async XLA Ops:
  0.0 1.7 %copy-start = (bf16[1536,768]{1,0:T(8,128)(2,1)S(1)}, bf16[1536,768]{1,0:T(8,128)(2,1)}, u32[]{:S(2)}) copy-start(bf16[1536,768]{1,0:T(8,128)(2,1)} %param.7) | copy-start | bytes 7077892
  22.5 1.3 %copy-start.2 = (bf16[8,64,768]{2,1,0:T(8,128)(2,1)}, bf16[8,64,768]{2,1,0:T(8,128)(2,1)S(1)}, u32[]{:S(2)}) copy-start(bf16[8,64,768]{2,1,0:T(8,128)(2,1)S(1)} %all_to_all.20) | copy-start | bytes 2359300
  22.5 12.8 %copy-start.5 = (s32[8]{0:T(128)S(1)}, s32[8]{0:T(128)}, u32[]{:S(2)}) copy-start(s32[8]{0:T(128)} %param.6) | copy-start | bytes 100
  23.8 34.3 %all-to-all-start.1 = ((bf16[32,16,768]{2,1,0:T(8,128)(2,1)}), bf16[32,16,768]{2,1,0:T(8,128)(2,1)}, u32[]{:S(2)}, u32[]{:S(2)}) async-start(bf16[32,16,768]{2,1,0:T(8,128)(2,1)} %copy.20), calls=%async_computation.1 | async-start | bytes 1572864 | tf_op jit(solution)/shard_map/all_to_all | solution.py:116
  81.9 26.4 %all-to-all-start.3 = ((bf16[32,16,768]{2,1,0:T(8,128)(2,1)}), bf16[32,16,768]{2,1,0:T(8,128)(2,1)S(1)}, u32[]{:S(2)}, u32[]{:S(2)}) async-start(bf16[32,16,768]{2,1,0:T(8,128)(2,1)} %bitcast.38), calls=%async_computation.3 | async-start | bytes 1572864 | tf_op jit(solution)/shard_map/all_to_all | solution.py:121
  108.5 1.4 %copy-start.1 = (f32[512,768]{1,0:T(8,128)S(1)}, f32[512,768]{1,0:T(8,128)}, u32[]{:S(2)}) copy-start(f32[512,768]{1,0:T(8,128)} %copy.27) | copy-start | bytes 4718596
  108.5 1.9 %copy-start.3 = (f32[512,768]{1,0:T(8,128)S(1)}, f32[512,768]{1,0:T(8,128)}, u32[]{:S(2)}) copy-start(f32[512,768]{1,0:T(8,128)} %get-tuple-element.9) | copy-start | bytes 4718596
  110.4 1.3 %copy-start.4 = (bf16[768,768]{1,0:T(8,128)(2,1)S(1)}, bf16[768,768]{1,0:T(8,128)(2,1)}, u32[]{:S(2)}) copy-start(bf16[768,768]{1,0:T(8,128)(2,1)} %param.9) | copy-start | bytes 3538948
